TPU v7x, 256 devices: a whole 4x4x8 slice. The times are simulated.
256 devices in a mesh: row: 8 (over x, y_lo), col: 32 (over y_hi, z, core).
Axes of the slice: x: 4, y: 4 (y_hi: 2, y_lo: 2; y = y_hi * 2 + y_lo), z: 8, core: 2. Of those that a mesh axis runs over, the one named last changes fastest.
Arguments:
- features: bfloat16 [65536, 128], P(('row', 'col')), may hold values from -6 to 6
- degrees: int32 [65536], P(('row', 'col')), may hold values from 32 to 159
- adj_tiles: bfloat16 [8, 32, 256, 4096], P('row', 'col'), may hold values from 0 to 0.22472483, as said below
- tile_rows: int32 [8, 32, 256], P('row', 'col'), may hold values from 0 to 127
- tile_cols: int32 [8, 32, 256], P('row', 'col'), may hold values from 0 to 31
- tile_counts: int32 [8, 32], P('row', 'col'), may hold values from 64 to 256, as said below
Outputs:
- propagated: bfloat16 [65536, 128], P(('row', 'col'))
Inputs may be any that keep to these rules, and one draw needn't show every extreme that they name: Each block holds at most 256 live tiles, in its first tile_counts slots; some block holds exactly 256. `adj_tiles`: edge weights are zero or positive.
All inputs are finite; a program needn't handle non-finite values.
Results may differ from a plain program's by a relative error of at most 0.0054.
Values may be sent and summed in bfloat16 or wider, within the bound.
A program may use at most 128 MiB of HBM per device.

v0:
```python
import jax
import jax.numpy as jnp
from jax import lax
from jax.sharding import PartitionSpec as P

TILE = 64
KNN = 32
STEPS = 2
ALPHA = 0.1


def shards(features, degrees, adj_tiles, tile_rows, tile_cols, tile_counts):
    col_count = lax.axis_size("col")
    nodes_dev = features.shape[0]
    feat_width = features.shape[1]
    tile_slots = adj_tiles.shape[2]
    dev_tiles = adj_tiles.reshape(tile_slots, TILE, TILE)
    row_ids_all = tile_rows.reshape(tile_slots)
    col_ids_all = tile_cols.reshape(tile_slots)
    live_count = tile_counts.reshape(())
    block_len = min(256, tile_slots)
    num_turns = tile_slots // block_len
    row_tiles = nodes_dev * col_count // TILE
    norm_scale = jnp.sqrt(KNN / degrees.astype(jnp.float32))[:, None]
    teleport = ALPHA * features.astype(jnp.float32)
    current = features.astype(jnp.float32)
    for repeat in range(STEPS):
        source = (norm_scale * current).astype(jnp.bfloat16)
        col_panel = lax.all_gather(source, "row", axis=0, tiled=True).reshape(-1, TILE, feat_width)

        def add_block(turn_index, totals):
            first_tile = turn_index * block_len
            live_mask = first_tile + jnp.arange(block_len, dtype=jnp.int32) < live_count
            inputs = col_panel[col_ids_all]
            products = jnp.einsum(
                "tab,tbf->taf", dev_tiles, inputs, preferred_element_type=jnp.float32
            )
            products = jnp.where(live_mask[:, None, None], products, jnp.zeros_like(products))
            return totals.at[row_ids_all].add(products)

        start_tot = jnp.zeros((row_tiles, TILE, feat_width), jnp.float32)
        totals = lax.fori_loop(0, num_turns, add_block, start_tot)
        partial_rows = totals.reshape(row_tiles * TILE, feat_width)
        own_rows = lax.psum_scatter(partial_rows, "col", scatter_dimension=0, tiled=True)
        current = (1.0 - ALPHA) * norm_scale * own_rows + teleport
    return current.astype(jnp.bfloat16)


def solution(mesh):
    return jax.shard_map(
        shards,
        mesh=mesh,
        in_specs=(
            P(("row", "col"), None),
            P(("row", "col")),
            P("row", "col", None, None),
            P("row", "col", None),
            P("row", "col", None),
            P("row", "col"),
        ),
        out_specs=P(("row", "col"), None),
        check_vma=False,
    )
```

profile of v0, /device:TPU:6, one launch (start us, length us, event | category | flops | bytes accessed | tf_op | source)
XLA Modules:
  0.0 449.4 jit_solution(6399208129320878904)
XLA Ops:
  6.5 0.0 reduce-scatter.3.cloned.1.call-start
  7.2 0.7 compare_select_fusion.1
  7.9 0.7 compare_select_fusion
  8.6 0.7 broadcast_multiply_fusion
  9.3 0.9 fusion.5
  10.2 28.9 %all_gather.6 = bf16[2048,128]{1,0:T(8,128)(2,1)S(1)} all-gather(bf16[256,128]{1,0:T(8,128)(2,1)S(1)} %fusion.5), channel_id=1, replica_groups=mesh['row'=8,'col'=32] {'row'}, dimensions={0}, use_global_device_ids=true | all-gather | bytes 589824 | tf_op jit(solution)/shard_map/all_gather | solution.py:29
  39.1 3.3 copy.7
  42.4 6.6 %copy.8 = bf16[256,64,64]{2,1,0:T(8,128)(2,1)} copy(bf16[256,64,64]{0,2,1:T(8,128)(2,1)S(1)} %bitcast.25) | data formatting | bytes 4194304 | tf_op jit(solution)/shard_map/reshape | solution.py:17
  49.0 3.0 gather_fusion
  52.1 7.9 %select_bitcast_fusion.1 = f32[256,64,128]{2,1,0:T(8,128)} fusion(pred[256]{0:T(512)(128)(4,1)S(1)} %iota_compare_fusion, bf16[256,64,64]{2,1,0:T(8,128)(2,1)} %copy.8, bf16[256,64,128]{2,1,0:T(8,128)(2,1)} %gather_fusion), kind=kOutput, calls=%fused_computation.5 | convolution fusion | flops 270532608 | bytes 14680320 | tf_op jit(solution)/shard_map/while/body/eval_jaxpr/tab,tbf->taf/dot_general | solution.py:35
  60.0 2.5 broadcast.71.clone
  62.5 39.3 %scatter_fusion = f32[128,64,128]{2,1,0:T(8,128)} fusion(f32[128,64,128]{2,1,0:T(8,128)} %broadcast.71.clone, s32[256]{0:T(256)S(1)} %bitcast.26, f32[256,64,128]{2,1,0:T(8,128)} %select_bitcast_fusion.1), kind=kCustom, calls=%fused_computation.2 | custom fusion | flops 2097152 | bytes 25166848 | tf_op jit(solution)/shard_map/while/body/eval_jaxpr/scatter-add | solution.py:39
  101.8 0.0 copy-start
  101.8 0.0 reduce-scatter.3.cloned.1.call-update
  101.8 0.0 reduce-scatter.5.cloned.1.call-start
  101.9 130.7 %reduce-scatter.3.cloned.1.call-done = f32[256,128]{1,0:T(8,128)} async-done(((f32[8192,128]{1,0:T(8,128)}), f32[256,128]{1,0:T(8,128)}) %reduce-scatter.3.cloned.1.call-update) | async-done | bytes 131088 | tf_op jit(solution)/shard_map/reduce_scatter | solution.py:44
  232.6 0.0 copy-done
  232.6 1.0 fusion.3
  233.6 26.8 %all_gather.7 = bf16[2048,128]{1,0:T(8,128)(2,1)S(1)} all-gather(bf16[256,128]{1,0:T(8,128)(2,1)S(1)} %fusion.3), channel_id=1, replica_groups=mesh['row'=8,'col'=32] {'row'}, dimensions={0}, use_global_device_ids=true | all-gather | bytes 589824 | tf_op jit(solution)/shard_map/all_gather | solution.py:29
  260.4 3.0 gather_fusion.1
  263.4 7.9 %select_bitcast_fusion = f32[256,64,128]{2,1,0:T(8,128)} fusion(pred[256]{0:T(512)(128)(4,1)S(1)} %iota_compare_fusion, bf16[256,64,64]{2,1,0:T(8,128)(2,1)} %copy.8, bf16[256,64,128]{2,1,0:T(8,128)(2,1)} %gather_fusion.1), kind=kOutput, calls=%fused_computation.4 | convolution fusion | flops 270532608 | bytes 14680320 | tf_op jit(solution)/shard_map/while/body/eval_jaxpr/tab,tbf->taf/dot_general | solution.py:35
  271.3 2.5 broadcast.71
  273.8 39.3 %scatter_fusion.1 = f32[128,64,128]{2,1,0:T(8,128)} fusion(f32[128,64,128]{2,1,0:T(8,128)} %broadcast.71, s32[256]{0:T(256)S(1)} %bitcast.27, f32[256,64,128]{2,1,0:T(8,128)} %select_bitcast_fusion), kind=kCustom, calls=%fused_computation.3 | custom fusion | flops 2097152 | bytes 25166848 | tf_op jit(solution)/shard_map/while/body/eval_jaxpr/scatter-add | solution.py:39
  313.2 0.0 reduce-scatter.5.cloned.1.call-update
  313.2 127.7 %reduce-scatter.5.cloned.1.call-done = f32[256,128]{1,0:T(8,128)} async-done(((f32[8192,128]{1,0:T(8,128)}), f32[256,128]{1,0:T(8,128)}) %reduce-scatter.5.cloned.1.call-update) | async-done | bytes 131088 | tf_op jit(solution)/shard_map/reduce_scatter | solution.py:44
  440.9 1.6 fusion.4
  (2 shorter events, 0.0 us)
Async XLA Ops:
  6.5 226.0 %reduce-scatter.3.cloned.1.call-start = ((), (), s32[]{:S(2)}) async-start(), calls=%async_computation.2 | async-start | bytes 4325376 | tf_op jit(solution)/shard_map/reduce_scatter | solution.py:44
  101.8 130.8 %copy-start = (bf16[256,128]{1,0:T(8,128)(2,1)S(1)}, bf16[256,128]{1,0:T(8,128)(2,1)}, u32[]{:S(2)}) copy-start(bf16[256,128]{1,0:T(8,128)(2,1)} %param.6) | copy-start | bytes 196612
  101.8 339.1 %reduce-scatter.5.cloned.1.call-start = ((), (), s32[]{:S(2)}) async-start(), calls=%async_computation.3 | async-start | bytes 4325376 | tf_op jit(solution)/shard_map/reduce_scatter | solution.py:44
Sparse Core Ops, SparseCore 0:
  101.9 130.5 reduce-scatter.2
  313.3 127.5 reduce-scatter.4
where the time goes:
time: 451 us; the launch traced here: 449 us
  waiting for transfers between devices  258 us (57%)
  other arithmetic  84.3 us (19%)
  blocking collectives  55.6 us (12%)
  local copies, waits for them, and re-layouts  21 us (5%)
  matrix products  15.9 us (4%)
  between operations  14.1 us (3%)
    reduce_scatter x2, waiting for transfers between devices, shards(): lax.psum_scatter(partial_rows, 'col', scatter_dimension=0, tiled=True)  258 us
    scatter-add x2, other arithmetic, add_block(): return totals.at[row_ids_all].add(products)  78.6 us
    all_gather x2, blocking collectives, shards(): lax.all_gather(source, 'row', axis=0, tiled=True)  55.6 us
    dot_general x2, matrix products, add_block(): jnp.einsum('tab,tbf->taf', dev_tiles, inputs, preferred_element_type=jnp....  15.9 us
  transfers between devices with their start and end apart: 2, of which 2 were waited for; matrix products, arithmetic and copies ran while one was open for 0% of the time, Pallas kernels for 0%

commit v1 on v0

--- a/solution.py
+++ b/solution.py
@@ -26,7 +26,9 @@
     current = features.astype(jnp.float32)
     for repeat in range(STEPS):
         source = (norm_scale * current).astype(jnp.bfloat16)
-        col_panel = lax.all_gather(source, "row", axis=0, tiled=True).reshape(-1, TILE, feat_width)
+        col_panel = jnp.concatenate(
+            lax.all_to_all(jnp.stack([source] * lax.axis_size("row")), "row", 0, 0), axis=0
+        ).reshape(-1, TILE, feat_width)
 
         def add_block(turn_index, totals):
             first_tile = turn_index * block_len

time: 451 us -> 411 us (0.911)
  blocking collectives: 55.6 us -> 10.9 us
  starting transfers between devices: 0.04 us -> 5.83 us
    all_gather x2 -> x0, blocking collectives: 55.6 us -> none  [shards(): lax.all_gather(source, 'row', axis=0, tiled=True)]
    all_to_all x0 -> x1, blocking collectives: none -> 10.9 us  [shards(): lax.all_to_all(jnp.stack([source] * lax.axis_size('row')), 'row', 0, 0)]
    all_to_all x0 -> x1, starting transfers between devices: none -> 5.79 us  [shards(): lax.all_to_all(jnp.stack([source] * lax.axis_size('row')), 'row', 0, 0)]
  transfers between devices with their start and end apart: 2 -> 3, of which waited for: 2 -> 2; matrix products, arithmetic and copies ran while one was open for 0% -> 3% of each run, Pallas kernels for 0% -> 0%
where the time goes in v1:
time: 411 us; the launch traced here: 410 us
  waiting for transfers between devices  257 us (63%)
  other arithmetic  83.6 us (20%)
  local copies, waits for them, and re-layouts  21.9 us (5%)
  matrix products  15.9 us (4%)
  between operations  14.1 us (3%)
  blocking collectives  10.9 us (3%)
  starting transfers between devices  5.83 us (1%)
    reduce_scatter x2, waiting for transfers between devices, shards(): lax.psum_scatter(partial_rows, 'col', scatter_dimension=0, tiled=True)  257 us
    scatter-add x2, other arithmetic, add_block(): return totals.at[row_ids_all].add(products)  78.6 us
    dot_general x2, matrix products, add_block(): jnp.einsum('tab,tbf->taf', dev_tiles, inputs, preferred_element_type=jnp....  15.9 us
    all_to_all x1, blocking collectives, shards(): lax.all_to_all(jnp.stack([source] * lax.axis_size('row')), 'row', 0, 0)  10.9 us
  transfers between devices with their start and end apart: 3, of which 2 were waited for; matrix products, arithmetic and copies ran while one was open for 3% of the time, Pallas kernels for 0%

profile of v1, /device:TPU:6, one launch (start us, length us, event | category | flops | bytes accessed | tf_op | source)
XLA Modules:
  0.0 409.5 jit_solution(1624326774405366969)
XLA Ops:
  6.5 0.7 broadcast_multiply_fusion
  7.2 0.9 fusion.5
  8.2 0.9 stack.4
  9.0 5.8 %all-to-all-start = ((bf16[8,256,128]{2,1,0:T(8,128)(2,1)}), bf16[8,256,128]{2,1,0:T(8,128)(2,1)S(1)}, u32[]{:S(2)}, u32[]{:S(2)}) async-start(bf16[8,256,128]{2,1,0:T(8,128)(2,1)} %stack.4), calls=%async_computation | async-start | bytes 1048576 | tf_op jit(solution)/shard_map/all_to_all | solution.py:30
  14.8 0.0 reduce-scatter.3.cloned.1.call-start
  14.8 0.7 compare_select_fusion
  16.2 3.3 copy.7
  19.4 0.0 copy-start.1
  19.5 6.6 %copy.8 = bf16[256,64,64]{2,1,0:T(8,128)(2,1)} copy(bf16[256,64,64]{0,2,1:T(8,128)(2,1)S(1)} %bitcast.25) | data formatting | bytes 4194304 | tf_op jit(solution)/shard_map/reshape | solution.py:17
  26.1 0.0 copy-done.1
  26.1 0.0 all-to-all-done
  26.1 3.1 gather_fusion
  29.2 7.9 %select_bitcast_fusion.1 = f32[256,64,128]{2,1,0:T(8,128)} fusion(pred[256]{0:T(512)(128)(4,1)S(1)} %iota_compare_fusion, bf16[256,64,64]{2,1,0:T(8,128)(2,1)} %copy.8, bf16[256,64,128]{2,1,0:T(8,128)(2,1)} %gather_fusion), kind=kOutput, calls=%fused_computation.5 | convolution fusion | flops 270532608 | bytes 14680320 | tf_op jit(solution)/shard_map/while/body/eval_jaxpr/tab,tbf->taf/dot_general | solution.py:37
  37.1 2.5 broadcast.75.clone
  39.6 39.3 %scatter_fusion = f32[128,64,128]{2,1,0:T(8,128)} fusion(f32[128,64,128]{2,1,0:T(8,128)} %broadcast.75.clone, s32[256]{0:T(256)S(1)} %bitcast.26, f32[256,64,128]{2,1,0:T(8,128)} %select_bitcast_fusion.1), kind=kCustom, calls=%fused_computation.2 | custom fusion | flops 2097152 | bytes 25166848 | tf_op jit(solution)/shard_map/while/body/eval_jaxpr/scatter-add | solution.py:41
  78.9 0.0 copy-start
  78.9 0.0 reduce-scatter.3.cloned.1.call-update
  78.9 0.0 reduce-scatter.5.cloned.1.call-start
  79.0 130.5 %reduce-scatter.3.cloned.1.call-done = f32[256,128]{1,0:T(8,128)} async-done(((f32[8192,128]{1,0:T(8,128)}), f32[256,128]{1,0:T(8,128)}) %reduce-scatter.3.cloned.1.call-update) | async-done | bytes 131088 | tf_op jit(solution)/shard_map/reduce_scatter | solution.py:46
  209.5 0.0 copy-done
  209.5 1.0 fusion.3
  210.6 0.1 stack.5
  210.6 10.9 %all_to_all.10 = bf16[8,256,128]{2,1,0:T(8,128)(2,1)S(1)} all-to-all(bf16[8,256,128]{2,1,0:T(8,128)(2,1)S(1)} %stack.5), channel_id=1, replica_groups=mesh['row'=8,'col'=32] {'row'}, dimensions={0} | all-to-all | bytes 1048576 | tf_op jit(solution)/shard_map/all_to_all | solution.py:30
  221.5 3.0 gather_fusion.1
  224.6 7.9 %select_bitcast_fusion = f32[256,64,128]{2,1,0:T(8,128)} fusion(pred[256]{0:T(512)(128)(4,1)S(1)} %iota_compare_fusion, bf16[256,64,64]{2,1,0:T(8,128)(2,1)} %copy.8, bf16[256,64,128]{2,1,0:T(8,128)(2,1)} %gather_fusion.1), kind=kOutput, calls=%fused_computation.4 | convolution fusion | flops 270532608 | bytes 14680320 | tf_op jit(solution)/shard_map/while/body/eval_jaxpr/tab,tbf->taf/dot_general | solution.py:37
  232.5 2.5 broadcast.75
  235.0 39.3 %scatter_fusion.1 = f32[128,64,128]{2,1,0:T(8,128)} fusion(f32[128,64,128]{2,1,0:T(8,128)} %broadcast.75, s32[256]{0:T(256)S(1)} %bitcast.27, f32[256,64,128]{2,1,0:T(8,128)} %select_bitcast_fusion), kind=kCustom, calls=%fused_computation.3 | custom fusion | flops 2097152 | bytes 25166848 | tf_op jit(solution)/shard_map/while/body/eval_jaxpr/scatter-add | solution.py:41
  274.3 0.0 reduce-scatter.5.cloned.1.call-update
  274.3 126.7 %reduce-scatter.5.cloned.1.call-done = f32[256,128]{1,0:T(8,128)} async-done(((f32[8192,128]{1,0:T(8,128)}), f32[256,128]{1,0:T(8,128)}) %reduce-scatter.5.cloned.1.call-update) | async-done | bytes 131088 | tf_op jit(solution)/shard_map/reduce_scatter | solution.py:46
  401.0 1.6 fusion.4
  (3 shorter events, 0.0 us)
Async XLA Ops:
  9.0 17.1 %all-to-all-start = ((bf16[8,256,128]{2,1,0:T(8,128)(2,1)}), bf16[8,256,128]{2,1,0:T(8,128)(2,1)S(1)}, u32[]{:S(2)}, u32[]{:S(2)}) async-start(bf16[8,256,128]{2,1,0:T(8,128)(2,1)} %stack.4), calls=%async_computation | async-start | bytes 1048576 | tf_op jit(solution)/shard_map/all_to_all | solution.py:30
  14.8 194.7 %reduce-scatter.3.cloned.1.call-start = ((), (), s32[]{:S(2)}) async-start(), calls=%async_computation.4 | async-start | bytes 4325376 | tf_op jit(solution)/shard_map/reduce_scatter | solution.py:46
  19.4 6.7 %copy-start.1 = (s32[1,1,256]{2,1,0:T(1,128)S(1)}, s32[1,1,256]{2,1,0:T(1,128)}, u32[]{:S(2)}) copy-start(s32[1,1,256]{2,1,0:T(1,128)} %param.9) | copy-start | bytes 3076
  78.9 130.6 %copy-start = (bf16[256,128]{1,0:T(8,128)(2,1)S(1)}, bf16[256,128]{1,0:T(8,128)(2,1)}, u32[]{:S(2)}) copy-start(bf16[256,128]{1,0:T(8,128)(2,1)} %param.6) | copy-start | bytes 196612
  78.9 322.1 %reduce-scatter.5.cloned.1.call-start = ((), (), s32[]{:S(2)}) async-start(), calls=%async_computation.5 | async-start | bytes 4325376 | tf_op jit(solution)/shard_map/reduce_scatter | solution.py:46
Sparse Core Ops, SparseCore 0:
  79.1 130.4 reduce-scatter.2
  274.4 126.5 reduce-scatter.4
